TPU v7x, 32 devices: a whole 2x2x4 slice. The times are simulated.
32 devices in a mesh: fiber: 8 (over z, core), group: 4 (over y, x).
Axes of the slice: x: 2, y: 2, z: 4, core: 2. Of those that a mesh axis runs over, the one named last changes fastest.
Arguments:
- field_slab: float32 [512, 64, 2048], P('fiber', 'group'), may hold values from -42 to 42
- start_basis: float32 [512, 128], replicated, may hold values from -6 to 6
Outputs:
- factor: float32 [512, 128], replicated
- core_slab: float32 [128, 64, 2048], P(None, 'group', 'fiber')
All inputs are finite; a program needn't handle non-finite values.
Results may differ from a plain program's by a relative error of at most 0.0003.
Values sent between devices are 32-bit elements; how exact they have to be, the bound alone decides.
No kernel may reach another device: no remote copies, remote signals or barrier semaphores. Data moves between devices by JAX's collectives and lax.ppermute only.
A program may use at most 128 MiB of HBM per device.

v0:
```python
import jax
import jax.numpy as jnp
from jax import lax
from jax.sharding import PartitionSpec as P

ITERS = 2
precise = lax.Precision.HIGHEST


def orthonormal(images):
    inner_products = jnp.dot(images.T, images, precision=precise)
    cholesky_factor = jnp.linalg.cholesky(inner_products)
    return lax.linalg.triangular_solve(
        cholesky_factor, images, left_side=False, lower=True, transpose_a=True
    )


def on_device(field_slab, start_basis):
    column_count = field_slab.shape[1] * field_slab.shape[2] * lax.axis_size("group")
    regrouped = lax.all_to_all(field_slab, "fiber", split_axis=2, concat_axis=0, tiled=True)
    columns = regrouped.reshape(regrouped.shape[0], regrouped.shape[1] * regrouped.shape[2])
    local_gram = jnp.dot(columns, columns.T, precision=precise)
    subspace = start_basis
    fiber_share = lax.psum_scatter(local_gram, "fiber", scatter_dimension=0, tiled=True)
    gram_share = lax.psum(fiber_share, "group") / column_count
    for iteration in range(ITERS):
        image_rows = jnp.dot(gram_share, subspace, precision=precise)
        subspace = orthonormal(lax.all_gather(image_rows, "fiber", axis=0, tiled=True))
    core_slab = jnp.einsum("mk,mbc->kbc", subspace, regrouped, precision=precise)
    return (subspace, core_slab)


def solution(mesh):
    return jax.shard_map(
        on_device,
        mesh=mesh,
        in_specs=(P("fiber", "group", None), P()),
        out_specs=(P(), P(None, "group", "fiber")),
        check_vma=False,
    )
```

profile of v0, /device:TPU:0, one launch (start us, length us, event | category | flops | bytes accessed | tf_op | source)
XLA Modules:
  0.0 485.6 jit_solution(11098625435497381214)
XLA Ops:
  7.2 15.6 %copy.22 = f32[64,16,2048]{0,1,2:T(8,128)} copy(f32[64,16,2048]{2,1,0:T(8,128)} %param.5) | data formatting | bytes 16777216 | tf_op args[0]
  22.8 15.4 %reshape.27 = f32[8,1,262144]{2,1,0:T(1,128)} reshape(f32[2048,16,64]{2,1,0:T(8,128)} %bitcast.49) | data formatting | bytes 16777216
  38.2 190.7 %all_to_all.18 = f32[8,1,262144]{2,1,0:T(1,128)} all-to-all(f32[8,1,262144]{2,1,0:T(1,128)} %reshape.27), channel_id=1, replica_groups=mesh['fiber'=8,'group'=4] {'fiber'}, dimensions={0} | all-to-all | bytes 16777216 | tf_op jit(solution)/shard_map/all_to_all | solution.py:20
  228.9 0.5 broadcast.36
  229.4 26.2 %reduce.4 = f32[8,262144]{1,0:T(8,128)} reduce(f32[8,1,262144]{2,1,0:T(1,128)} %all_to_all.18, f32[]{:T(128)} %broadcast.36), dimensions={1}, to_apply=%all_to_all.13.reduce_sub_computation | reduce | bytes 16777220 | tf_op jit(solution)/shard_map/all_to_all | solution.py:20
  255.7 15.6 %reshape.28 = f32[2048,16,64]{2,1,0:T(8,128)} reshape(f32[8,262144]{1,0:T(8,128)} %reduce.4) | data formatting | bytes 16777216
  271.3 15.8 %copy.23 = f32[64,16,8,256]{3,1,0,2:T(8,128)} copy(f32[64,16,8,256]{0,1,3,2:T(8,128)} %bitcast.47) | data formatting | bytes 16777216 | tf_op jit(solution)/shard_map/all_to_all | solution.py:20
  287.0 11.5 %copy.30 = f32[64,8,16,256]{3,1,2,0:T(8,128)S(1)} copy(f32[64,8,16,256]{3,2,1,0:T(8,128)} %bitcast.51) | data formatting | bytes 16777216
  298.5 14.9 %fusion.19 = f32[512,512]{1,0:T(8,128)} fusion(f32[512,4096]{1,0:T(8,128)S(1)} %bitcast.46), kind=kOutput, calls=%fused_computation.29 | convolution fusion | flops 12884901888 | bytes 9437184 | tf_op jit(solution)/shard_map/dot_general | solution.py:22
  313.5 32.2 %reduce-scatter.2.cloned.1.call-done = f32[64,512]{1,0:T(8,128)} async-done(((f32[512,512]{1,0:T(8,128)}), f32[64,512]{1,0:T(8,128)}) %reduce-scatter.2.cloned.1.call-update) | async-done | bytes 131088 | tf_op jit(solution)/shard_map/reduce_scatter | solution.py:24
  345.7 12.8 %copy.26 = f32[8,64,16,256]{3,1,0,2:T(8,128)} copy(f32[8,64,16,256]{1,2,3,0:T(8,128)} %bitcast.48) | data formatting | bytes 16777216 | tf_op jit(solution)/shard_map/all_to_all | solution.py:20
  358.5 30.5 %all-reduce.2.cloned.1.call-done = f32[64,512]{1,0:T(8,128)} async-done(((f32[64,512]{1,0:T(8,128)}), f32[64,512]{1,0:T(8,128)}) %all-reduce.2.cloned.1.call-update) | async-done | bytes 131088 | tf_op jit(solution)/shard_map/psum | solution.py:25
  389.0 1.2 fusion.4
  390.2 14.3 %all_gather.6 = f32[512,128]{1,0:T(8,128)S(1)} all-gather(f32[64,128]{1,0:T(8,128)S(1)} %fusion.4), channel_id=1, replica_groups=mesh['fiber'=8,'group'=4] {'fiber'}, dimensions={0}, use_global_device_ids=true | all-gather | bytes 294912 | tf_op jit(solution)/shard_map/all_gather | solution.py:28
  404.5 0.6 fusion.20
  405.2 11.7 %cholesky.44 = f32[128,128]{1,0:T(8,128)S(1)} custom-call(f32[128,128]{1,0:T(8,128)S(1)} %fusion.12), custom_call_target="Cholesky" | custom-call | tf_op jit(solution)/shard_map/jit(cholesky)/cholesky | solution.py:12
  416.9 0.6 compare_reduce_fusion.1
  417.6 0.7 fusion.6
  418.2 9.8 %custom-call.6 = f32[1,128,128]{1,2,0:T(8,128)S(1)} custom-call(f32[1,128,128]{2,1,0:T(8,128)S(1)} %fusion.6), custom_call_target="InvertDiagBlocksLowerTriangular" | custom-call | tf_op jit(solution)/shard_map/triangular_solve/custom-call.0 | solution.py:13
  428.0 0.4 convolution_bitcast_fusion
  428.5 1.3 fusion.2
  429.8 14.4 %all_gather.7 = f32[512,128]{1,0:T(8,128)S(1)} all-gather(f32[64,128]{1,0:T(8,128)S(1)} %fusion.2), channel_id=1, replica_groups=mesh['fiber'=8,'group'=4] {'fiber'}, dimensions={0}, use_global_device_ids=true | all-gather | bytes 294912 | tf_op jit(solution)/shard_map/all_gather | solution.py:28
  444.2 0.6 fusion.21
  444.8 0.1 copy.25
  444.9 11.7 %cholesky.55 = f32[128,128]{1,0:T(8,128)S(1)} custom-call(f32[128,128]{1,0:T(8,128)S(1)} %fusion.10), custom_call_target="Cholesky" | custom-call | tf_op jit(solution)/shard_map/jit(cholesky)/cholesky | solution.py:12
  456.7 0.6 compare_reduce_fusion
  457.3 0.7 fusion.7
  458.0 9.8 %custom-call.7 = f32[1,128,128]{1,2,0:T(8,128)S(1)} custom-call(f32[1,128,128]{2,1,0:T(8,128)S(1)} %fusion.7), custom_call_target="InvertDiagBlocksLowerTriangular" | custom-call | tf_op jit(solution)/shard_map/triangular_solve/custom-call.0 | solution.py:13
  467.8 0.4 fusion.8
  468.2 0.8 copy.27
  469.1 6.9 %fusion = f32[128,16,256]{2,0,1:T(8,128)S(1)} fusion(f32[512,16,256]{2,0,1:T(8,128)} %bitcast.50, f32[128,512]{1,0:T(8,128)S(1)} %fusion.8), kind=kOutput, calls=%fused_computation.1 | convolution fusion | flops 3221225472 | bytes 10747904 | tf_op jit(solution)/shard_map/mk,mbc->kbc/dot_general | solution.py:29
  476.0 2.5 copy.28
  (11 shorter events, 0.3 us)
Async XLA Ops:
  7.2 381.9 %copy-start = (f32[512,128]{1,0:T(8,128)S(1)}, f32[512,128]{1,0:T(8,128)}, u32[]{:S(2)}) copy-start(f32[512,128]{1,0:T(8,128)} %param.6) | copy-start | bytes 786436
  7.2 338.5 %reduce-scatter.2.cloned.1.call-start = ((), (), s32[]{:S(2)}) async-start(), calls=%async_computation.2 | async-start | bytes 1179648 | tf_op jit(solution)/shard_map/reduce_scatter | solution.py:24
  313.5 75.5 %all-reduce.2.cloned.1.call-start = ((), (), s32[]{:S(2)}) async-start(), calls=%async_computation.3 | async-start | bytes 262144 | tf_op jit(solution)/shard_map/psum | solution.py:25
Sparse Core Ops, SparseCore 0:
  313.6 32.0 reduce-scatter.1
  348.6 40.4 all-reduce.1
where the time goes:
time: 489 us; the launch traced here: 486 us
  blocking collectives  219 us (45%)
  local copies, waits for them, and re-layouts  90.7 us (19%)
  other arithmetic  72 us (15%)
  waiting for transfers between devices  62.7 us (13%)
  matrix products  26.3 us (5%)
  between operations  14.4 us (3%)
    all_to_all x1, blocking collectives, on_device(): lax.all_to_all(field_slab, 'fiber', split_axis=2, concat_axis=0, tiled=True)  191 us
    unnamed x8, local copies, waits for them, and re-layouts  61.4 us
    reduce_scatter x1, waiting for transfers between devices, on_device(): lax.psum_scatter(local_gram, 'fiber', scatter_dimension=0, tiled=True)  32.2 us
    psum x1, waiting for transfers between devices, on_device(): gram_share = lax.psum(fiber_share, 'group') / column_count  30.5 us
    all_to_all x3, local copies, waits for them, and re-layouts, on_device(): lax.all_to_all(field_slab, 'fiber', split_axis=2, concat_axis=0, tiled=True)  29.1 us
    all_gather x2, blocking collectives, on_device(): lax.all_gather(image_rows, 'fiber', axis=0, tiled=True)  28.7 us
    all_to_all x1, other arithmetic, on_device(): lax.all_to_all(field_slab, 'fiber', split_axis=2, concat_axis=0, tiled=True)  26.2 us
    another operation x6, other arithmetic, orthonormal(): cholesky_factor = jnp.linalg.cholesky(inner_products)  24.8 us
  transfers between devices with their start and end apart: 2, of which 2 were waited for; matrix products, arithmetic and copies ran while one was open for 3% of the time, Pallas kernels for 0%

commit v1 on v0

--- a/solution.py
+++ b/solution.py
@@ -5,6 +5,28 @@
 
 ITERS = 2
 precise = lax.Precision.HIGHEST
+
+
+def joined_along(pieces, dim):
+    pieces = jnp.moveaxis(pieces, 0, dim)
+    shape = pieces.shape
+    return pieces.reshape(*shape[:dim], shape[dim] * shape[dim + 1], *shape[dim + 2 :])
+
+
+def gather_around(x, axis, dim):
+    size = lax.axis_size(axis)
+    pairs = [(i, (i + 1) % size) for i in range(size)]
+    back = [(b, a) for a, b in pairs]
+    lower, upper = ([], [])
+    for step in range(size - 1):
+        if step % 2 == 0:
+            lower.append(lax.ppermute(lower[-1] if lower else x, axis, pairs))
+        else:
+            upper.append(lax.ppermute(upper[-1] if upper else x, axis, back))
+    blocks = jnp.stack([*lower[::-1], x, *upper])
+    shift = lax.axis_index(axis) - len(lower)
+    blocks = blocks[(jnp.arange(size) - shift) % size]
+    return joined_along(blocks, dim)
 
 
 def orthonormal(images):
@@ -25,7 +47,7 @@
     gram_share = lax.psum(fiber_share, "group") / column_count
     for iteration in range(ITERS):
         image_rows = jnp.dot(gram_share, subspace, precision=precise)
-        subspace = orthonormal(lax.all_gather(image_rows, "fiber", axis=0, tiled=True))
+        subspace = orthonormal(gather_around(image_rows, "fiber", 0))
     core_slab = jnp.einsum("mk,mbc->kbc", subspace, regrouped, precision=precise)
     return (subspace, core_slab)
 

time: 489 us -> 516 us (1.055)
  waiting for transfers between devices: 62.7 us -> 95.6 us
  blocking collectives: 219 us -> 191 us
  starting transfers between devices: 0.08 us -> 22 us
    all_gather x2 -> x0, blocking collectives: 28.7 us -> none  [on_device(): lax.all_gather(image_rows, 'fiber', axis=0, tiled=True)]
    ppermute x0 -> x14, starting transfers between devices: none -> 21.9 us  [the longest x6 21.8 us: gather_around(): upper.append(lax.ppermute(upper[-1] if upper else x, axis, back))]
    ppermute x0 -> x14, waiting for transfers between devices: none -> 20.1 us  [the longest x8 18.3 us: gather_around(): lower.append(lax.ppermute(lower[-1] if lower else x, axis, pairs))]
    psum x1, waiting for transfers between devices: 30.5 us -> 43.3 us  [on_device(): gram_share = lax.psum(fiber_share, 'group') / column_count]
    unnamed x8 -> x22, local copies, waits for them, and re-layouts: 61.4 us -> 61.5 us
  transfers between devices with their start and end apart: 2 -> 16, of which waited for: 2 -> 11; matrix products, arithmetic and copies ran while one was open for 3% -> 3% of each run, Pallas kernels for 0% -> 0%
where the time goes in v1:
time: 516 us; the launch traced here: 513 us
  blocking collectives  191 us (37%)
  waiting for transfers between devices  95.6 us (19%)
  local copies, waits for them, and re-layouts  91.5 us (18%)
  other arithmetic  72 us (14%)
  matrix products  26.2 us (5%)
  starting transfers between devices  22 us (4%)
  between operations  14.6 us (3%)
    all_to_all x1, blocking collectives, on_device(): lax.all_to_all(field_slab, 'fiber', split_axis=2, concat_axis=0, tiled=True)  191 us
    unnamed x22, local copies, waits for them, and re-layouts  61.5 us
    psum x1, waiting for transfers between devices, on_device(): gram_share = lax.psum(fiber_share, 'group') / column_count  43.3 us
    reduce_scatter x1, waiting for transfers between devices, on_device(): lax.psum_scatter(local_gram, 'fiber', scatter_dimension=0, tiled=True)  32.3 us
    all_to_all x3, local copies, waits for them, and re-layouts, on_device(): lax.all_to_all(field_slab, 'fiber', split_axis=2, concat_axis=0, tiled=True)  28.7 us
    all_to_all x1, other arithmetic, on_device(): lax.all_to_all(field_slab, 'fiber', split_axis=2, concat_axis=0, tiled=True)  26.2 us
    another operation x6, other arithmetic, orthonormal(): cholesky_factor = jnp.linalg.cholesky(inner_products)  24.8 us
    ppermute x6, starting transfers between devices, gather_around(): upper.append(lax.ppermute(upper[-1] if upper else x, axis, back))  21.8 us
  transfers between devices with their start and end apart: 16, of which 11 were waited for; matrix products, arithmetic and copies ran while one was open for 3% of the time, Pallas kernels for 0%

profile of v1, /device:TPU:0, one launch (start us, length us, event | category | flops | bytes accessed | tf_op | source)
XLA Modules:
  0.0 512.8 jit_solution(7434897409822934454)
XLA Ops:
  7.2 15.5 %copy.22 = f32[64,16,2048]{0,1,2:T(8,128)} copy(f32[64,16,2048]{2,1,0:T(8,128)} %param.5) | data formatting | bytes 16777216 | tf_op args[0]
  22.8 15.4 %reshape.102 = f32[8,1,262144]{2,1,0:T(1,128)} reshape(f32[2048,16,64]{2,1,0:T(8,128)} %bitcast.89) | data formatting | bytes 16777216
  38.2 190.9 %all_to_all.18 = f32[8,1,262144]{2,1,0:T(1,128)} all-to-all(f32[8,1,262144]{2,1,0:T(1,128)} %reshape.102), channel_id=1, replica_groups=mesh['fiber'=8,'group'=4] {'fiber'}, dimensions={0} | all-to-all | bytes 16777216 | tf_op jit(solution)/shard_map/all_to_all | solution.py:42
  229.6 26.2 %reduce.4 = f32[8,262144]{1,0:T(8,128)} reduce(f32[8,1,262144]{2,1,0:T(1,128)} %all_to_all.18, f32[]{:T(128)} %broadcast.108), dimensions={1}, to_apply=%all_to_all.13.reduce_sub_computation | reduce | bytes 16777220 | tf_op jit(solution)/shard_map/all_to_all | solution.py:42
  255.8 15.6 %reshape.103 = f32[2048,16,64]{2,1,0:T(8,128)} reshape(f32[8,262144]{1,0:T(8,128)} %reduce.4) | data formatting | bytes 16777216
  271.5 15.4 %copy.23 = f32[64,16,8,256]{3,1,0,2:T(8,128)} copy(f32[64,16,8,256]{0,1,3,2:T(8,128)} %bitcast.87) | data formatting | bytes 16777216 | tf_op jit(solution)/shard_map/all_to_all | solution.py:42
  286.9 11.5 %copy.30 = f32[64,8,16,256]{3,1,2,0:T(8,128)S(1)} copy(f32[64,8,16,256]{3,2,1,0:T(8,128)} %bitcast.91) | data formatting | bytes 16777216
  298.4 14.7 %fusion.21 = f32[512,512]{1,0:T(8,128)} fusion(f32[512,4096]{1,0:T(8,128)S(1)} %bitcast.86), kind=kOutput, calls=%fused_computation.56 | convolution fusion | flops 12884901888 | bytes 9437184 | tf_op jit(solution)/shard_map/dot_general | solution.py:44
  313.2 32.3 %reduce-scatter.2.cloned.1.call-done = f32[64,512]{1,0:T(8,128)} async-done(((f32[512,512]{1,0:T(8,128)}), f32[64,512]{1,0:T(8,128)}) %reduce-scatter.2.cloned.1.call-update) | async-done | bytes 131088 | tf_op jit(solution)/shard_map/reduce_scatter | solution.py:46
  345.5 43.3 %all-reduce.2.cloned.1.call-done = f32[64,512]{1,0:T(8,128)} async-done(((f32[64,512]{1,0:T(8,128)}), f32[64,512]{1,0:T(8,128)}) %all-reduce.2.cloned.1.call-update) | async-done | bytes 131088 | tf_op jit(solution)/shard_map/psum | solution.py:47
  390.0 5.1 collective-permute-done
  395.1 3.5 collective-permute-start.4
  398.7 1.9 collective-permute-done.1
  400.6 3.6 collective-permute-start.5
  404.2 1.6 collective-permute-done.2
  405.8 3.8 collective-permute-start.6
  409.6 1.3 collective-permute-done.3
  412.5 11.7 %cholesky.44 = f32[128,128]{1,0:T(8,128)S(1)} custom-call(f32[128,128]{1,0:T(8,128)S(1)} %fusion.12), custom_call_target="Cholesky" | custom-call | tf_op jit(solution)/shard_map/jit(cholesky)/cholesky | solution.py:34
  425.5 9.8 %custom-call.6 = f32[1,128,128]{1,2,0:T(8,128)S(1)} custom-call(f32[1,128,128]{2,1,0:T(8,128)S(1)} %fusion.6), custom_call_target="InvertDiagBlocksLowerTriangular" | custom-call | tf_op jit(solution)/shard_map/triangular_solve/custom-call.0 | solution.py:35
  435.8 1.3 fusion.2
  437.1 5.1 collective-permute-done.7
  442.3 3.5 collective-permute-start.11
  445.8 1.7 collective-permute-done.8
  447.5 3.5 collective-permute-start.12
  451.0 1.6 collective-permute-done.9
  452.6 12.7 %copy.26 = f32[8,64,16,256]{3,1,0,2:T(8,128)} copy(f32[8,64,16,256]{1,2,3,0:T(8,128)} %bitcast.88) | data formatting | bytes 16777216 | tf_op jit(solution)/shard_map/all_to_all | solution.py:42
  465.4 3.8 collective-permute-start.13
  469.2 1.5 collective-permute-done.13
  472.0 11.7 %cholesky.55 = f32[128,128]{1,0:T(8,128)S(1)} custom-call(f32[128,128]{1,0:T(8,128)S(1)} %fusion.10), custom_call_target="Cholesky" | custom-call | tf_op jit(solution)/shard_map/jit(cholesky)/cholesky | solution.py:34
  485.1 9.8 %custom-call.7 = f32[1,128,128]{1,2,0:T(8,128)S(1)} custom-call(f32[1,128,128]{2,1,0:T(8,128)S(1)} %fusion.7), custom_call_target="InvertDiagBlocksLowerTriangular" | custom-call | tf_op jit(solution)/shard_map/triangular_solve/custom-call.0 | solution.py:35
  495.3 6.9 %fusion = f32[128,16,256]{2,0,1:T(8,128)S(1)} fusion(f32[512,16,256]{2,0,1:T(8,128)} %bitcast.90, f32[128,512]{1,0:T(8,128)S(1)} %fusion.8), kind=kOutput, calls=%fused_computation.5 | convolution fusion | flops 3221225472 | bytes 10747904 | tf_op jit(solution)/shard_map/mk,mbc->kbc/dot_general | solution.py:51
  502.3 2.5 copy.28
  (57 shorter events, 9.1 us)
Async XLA Ops:
  7.2 381.6 %copy-start = (f32[512,128]{1,0:T(8,128)S(1)}, f32[512,128]{1,0:T(8,128)}, u32[]{:S(2)}) copy-start(f32[512,128]{1,0:T(8,128)} %param.6) | copy-start | bytes 786436
  7.2 338.3 %reduce-scatter.2.cloned.1.call-start = ((), (), s32[]{:S(2)}) async-start(), calls=%async_computation.2 | async-start | bytes 1179648 | tf_op jit(solution)/shard_map/reduce_scatter | solution.py:46
  313.2 75.6 %all-reduce.2.cloned.1.call-start = ((), (), s32[]{:S(2)}) async-start(), calls=%async_computation.3 | async-start | bytes 262144 | tf_op jit(solution)/shard_map/psum | solution.py:47
  389.9 5.2 %collective-permute-start = (f32[64,128]{1,0:T(8,128)S(1)}, f32[64,128]{1,0:T(8,128)S(1)}, u32[]{:S(2)}, u32[]{:S(2)}) collective-permute-start(f32[64,128]{1,0:T(8,128)S(1)} %fusion.4), channel_id=1, source_target_pairs={{0,4},{4,8},{8,12},{12,16},{16,20},{20,24},{24,28},{28,0},{1,5},{5... | collective-permute-start | bytes 98312 | tf_op jit(solution)/shard_map/ppermute | solution.py:23
  395.1 5.5 %collective-permute-start.1 = (f32[64,128]{1,0:T(8,128)S(1)}, f32[64,128]{1,0:T(8,128)S(1)}, u32[]{:S(2)}, u32[]{:S(2)}) collective-permute-start(f32[64,128]{1,0:T(8,128)S(1)} %collective-permute-done), channel_id=1, source_target_pairs={{0,4},{4,8},{8,12},{12,16},{16,20},{20,24},{24,28},{28,0},{1,5},{5... | collective-permute-start | bytes 98312 | tf_op jit(solution)/shard_map/ppermute | solution.py:23
  395.1 5.5 %collective-permute-start.4 = (f32[64,128]{1,0:T(8,128)S(1)}, f32[64,128]{1,0:T(8,128)S(1)}, u32[]{:S(2)}, u32[]{:S(2)}) collective-permute-start(f32[64,128]{1,0:T(8,128)S(1)} %fusion.4), channel_id=1, source_target_pairs={{4,0},{8,4},{12,8},{16,12},{20,16},{24,20},{28,24},{0,28},{5,1},{9... | collective-permute-start | bytes 98312 | tf_op jit(solution)/shard_map/ppermute | solution.py:25
  400.6 5.2 %collective-permute-start.2 = (f32[64,128]{1,0:T(8,128)S(1)}, f32[64,128]{1,0:T(8,128)S(1)}, u32[]{:S(2)}, u32[]{:S(2)}) collective-permute-start(f32[64,128]{1,0:T(8,128)S(1)} %collective-permute-done.1), channel_id=1, source_target_pairs={{0,4},{4,8},{8,12},{12,16},{16,20},{20,24},{24,28},{28,0},{1,5},{5... | collective-permute-start | bytes 98312 | tf_op jit(solution)/shard_map/ppermute | solution.py:23
  400.6 5.2 %collective-permute-start.5 = (f32[64,128]{1,0:T(8,128)S(1)}, f32[64,128]{1,0:T(8,128)S(1)}, u32[]{:S(2)}, u32[]{:S(2)}) collective-permute-start(f32[64,128]{1,0:T(8,128)S(1)} %collective-permute-done.4), channel_id=1, source_target_pairs={{4,0},{8,4},{12,8},{16,12},{20,16},{24,20},{28,24},{0,28},{5,1},{9... | collective-permute-start | bytes 98312 | tf_op jit(solution)/shard_map/ppermute | solution.py:25
  405.8 5.1 %collective-permute-start.3 = (f32[64,128]{1,0:T(8,128)S(1)}, f32[64,128]{1,0:T(8,128)S(1)}, u32[]{:S(2)}, u32[]{:S(2)}) collective-permute-start(f32[64,128]{1,0:T(8,128)S(1)} %collective-permute-done.2), channel_id=1, source_target_pairs={{0,4},{4,8},{8,12},{12,16},{16,20},{20,24},{24,28},{28,0},{1,5},{5... | collective-permute-start | bytes 98312 | tf_op jit(solution)/shard_map/ppermute | solution.py:23
  405.8 5.4 %collective-permute-start.6 = (f32[64,128]{1,0:T(8,128)S(1)}, f32[64,128]{1,0:T(8,128)S(1)}, u32[]{:S(2)}, u32[]{:S(2)}) collective-permute-start(f32[64,128]{1,0:T(8,128)S(1)} %collective-permute-done.5), channel_id=1, source_target_pairs={{4,0},{8,4},{12,8},{16,12},{20,16},{24,20},{28,24},{0,28},{5,1},{9... | collective-permute-start | bytes 98312 | tf_op jit(solution)/shard_map/ppermute | solution.py:25
  437.1 5.2 %collective-permute-start.7 = (f32[64,128]{1,0:T(8,128)S(1)}, f32[64,128]{1,0:T(8,128)S(1)}, u32[]{:S(2)}, u32[]{:S(2)}) collective-permute-start(f32[64,128]{1,0:T(8,128)S(1)} %fusion.2), channel_id=1, source_target_pairs={{0,4},{4,8},{8,12},{12,16},{16,20},{20,24},{24,28},{28,0},{1,5},{5... | collective-permute-start | bytes 98312 | tf_op jit(solution)/shard_map/ppermute | solution.py:23
  442.3 5.2 %collective-permute-start.8 = (f32[64,128]{1,0:T(8,128)S(1)}, f32[64,128]{1,0:T(8,128)S(1)}, u32[]{:S(2)}, u32[]{:S(2)}) collective-permute-start(f32[64,128]{1,0:T(8,128)S(1)} %collective-permute-done.7), channel_id=1, source_target_pairs={{0,4},{4,8},{8,12},{12,16},{16,20},{20,24},{24,28},{28,0},{1,5},{5... | collective-permute-start | bytes 98312 | tf_op jit(solution)/shard_map/ppermute | solution.py:23
  442.3 5.2 %collective-permute-start.11 = (f32[64,128]{1,0:T(8,128)S(1)}, f32[64,128]{1,0:T(8,128)S(1)}, u32[]{:S(2)}, u32[]{:S(2)}) collective-permute-start(f32[64,128]{1,0:T(8,128)S(1)} %fusion.2), channel_id=1, source_target_pairs={{4,0},{8,4},{12,8},{16,12},{20,16},{24,20},{28,24},{0,28},{5,1},{9... | collective-permute-start | bytes 98312 | tf_op jit(solution)/shard_map/ppermute | solution.py:25
  447.5 5.1 %collective-permute-start.9 = (f32[64,128]{1,0:T(8,128)S(1)}, f32[64,128]{1,0:T(8,128)S(1)}, u32[]{:S(2)}, u32[]{:S(2)}) collective-permute-start(f32[64,128]{1,0:T(8,128)S(1)} %collective-permute-done.8), channel_id=1, source_target_pairs={{0,4},{4,8},{8,12},{12,16},{16,20},{20,24},{24,28},{28,0},{1,5},{5... | collective-permute-start | bytes 98312 | tf_op jit(solution)/shard_map/ppermute | solution.py:23
  447.5 17.9 %collective-permute-start.12 = (f32[64,128]{1,0:T(8,128)S(1)}, f32[64,128]{1,0:T(8,128)S(1)}, u32[]{:S(2)}, u32[]{:S(2)}) collective-permute-start(f32[64,128]{1,0:T(8,128)S(1)} %collective-permute-done.11), channel_id=1, source_target_pairs={{4,0},{8,4},{12,8},{16,12},{20,16},{24,20},{28,24},{0,28},{5,1},{9... | collective-permute-start | bytes 98312 | tf_op jit(solution)/shard_map/ppermute | solution.py:25
  452.6 16.5 %collective-permute-start.10 = (f32[64,128]{1,0:T(8,128)S(1)}, f32[64,128]{1,0:T(8,128)S(1)}, u32[]{:S(2)}, u32[]{:S(2)}) collective-permute-start(f32[64,128]{1,0:T(8,128)S(1)} %collective-permute-done.9), channel_id=1, source_target_pairs={{0,4},{4,8},{8,12},{12,16},{16,20},{20,24},{24,28},{28,0},{1,5},{5... | collective-permute-start | bytes 98312 | tf_op jit(solution)/shard_map/ppermute | solution.py:23
  465.4 5.4 %collective-permute-start.13 = (f32[64,128]{1,0:T(8,128)S(1)}, f32[64,128]{1,0:T(8,128)S(1)}, u32[]{:S(2)}, u32[]{:S(2)}) collective-permute-start(f32[64,128]{1,0:T(8,128)S(1)} %collective-permute-done.12), channel_id=1, source_target_pairs={{4,0},{8,4},{12,8},{16,12},{20,16},{24,20},{28,24},{0,28},{5,1},{9... | collective-permute-start | bytes 98312 | tf_op jit(solution)/shard_map/ppermute | solution.py:25
Sparse Core Ops, SparseCore 0:
  313.3 32.1 reduce-scatter.1
  348.3 40.3 all-reduce.1
